TPU v7x, 32 devices: a whole 2x2x4 slice. The times are simulated.
32 devices in a mesh: row: 2 (over y), col: 16 (over z, x, core).
Axes of the slice: x: 2, y: 2, z: 4, core: 2. Of those that a mesh axis runs over, the one named last changes fastest.
Arguments:
- tokens: bfloat16 [25088, 1024], P(('col', 'row')), may hold values from -6 to 6
- w_qkv: bfloat16 [1024, 3072], P('row', 'col'), may hold values from -0.1875 to 0.1875
- w_proj: bfloat16 [1024, 1024], P('row', 'col'), may hold values from -6 to 6
- w_fc1: bfloat16 [1024, 4096], P('row', 'col'), may hold values from -0.1875 to 0.1875
- w_fc2: bfloat16 [4096, 1024], P('row', 'col'), may hold values from -0.09375 to 0.09375
- ln1_gain: bfloat16 [1024], P(('col', 'row')), may hold values from 0.099609375 to 1.8984375
- ln1_bias: bfloat16 [1024], P(('col', 'row')), may hold values from -6 to 6
- q_bias: bfloat16 [1024], P(('col', 'row')), may hold values from -6 to 6
- v_bias: bfloat16 [1024], P(('col', 'row')), may hold values from -0.4375 to 0.4375
- proj_bias: bfloat16 [1024], P(('col', 'row')), may hold values from -6 to 6
- ln2_gain: bfloat16 [1024], P(('col', 'row')), may hold values from 0.099609375 to 1.8984375
- ln2_bias: bfloat16 [1024], P(('col', 'row')), may hold values from -6 to 6
- fc1_bias: bfloat16 [4096], P(('col', 'row')), may hold values from -6 to 6
- fc2_bias: bfloat16 [1024], P(('col', 'row')), may hold values from -6 to 6
- cotangent: float32 [25088, 1024], P(('col', 'row')), may hold values from -6 to 6
Outputs:
- output: bfloat16 [25088, 1024], P(('col', 'row'))
- grad_tokens: float32 [25088, 1024], P(('col', 'row'))
- grad_qkv: float32 [1024, 3072], P('row', 'col')
- grad_proj: float32 [1024, 1024], P('row', 'col')
- grad_fc1: float32 [1024, 4096], P('row', 'col')
- grad_fc2: float32 [4096, 1024], P('row', 'col')
- grad_ln1_gain: float32 [1024], P(('col', 'row'))
- grad_ln1_bias: float32 [1024], P(('col', 'row'))
- grad_q_bias: float32 [1024], P(('col', 'row'))
- grad_v_bias: float32 [1024], P(('col', 'row'))
- grad_proj_bias: float32 [1024], P(('col', 'row'))
- grad_ln2_gain: float32 [1024], P(('col', 'row'))
- grad_ln2_bias: float32 [1024], P(('col', 'row'))
- grad_fc1_bias: float32 [4096], P(('col', 'row'))
- grad_fc2_bias: float32 [1024], P(('col', 'row'))
All inputs are finite; a program needn't handle non-finite values.
Results may differ from a plain program's by a relative error of at most 0.019.
Values may be sent and summed in bfloat16 or wider, within the bound.
No kernel may reach another device: no remote copies, remote signals or barrier semaphores. Data moves between devices by JAX's collectives and lax.ppermute only.
A program may use at most 448 MiB of HBM per device.

v0:
```python
import math
import jax
import jax.numpy as jnp
from jax import lax
from jax.sharding import PartitionSpec as P

D = 1024
H = 16
HD = 64
LEN = 1568
EPSILON = 1e-06


def layer_norm(value, gain, shift):
    average = jnp.mean(value, axis=-1, keepdims=True)
    centred = value - average
    spread = jnp.mean(centred * centred, axis=-1, keepdims=True)
    inverse = lax.rsqrt(spread + EPSILON)
    normed = centred * inverse
    return (normed * gain + shift, normed, inverse)


def norm_back(grad_out, normed, inverse, gain):
    scaled = grad_out * gain
    mean_first = jnp.mean(scaled, axis=-1, keepdims=True)
    mean_second = jnp.mean(scaled * normed, axis=-1, keepdims=True)
    return inverse * (scaled - mean_first - normed * mean_second)


def gelu_slope(pre_act):
    cumulative = 0.5 * (1.0 + lax.erf(pre_act * 2.0 ** (-0.5)))
    density = jnp.exp(-0.5 * pre_act * pre_act) * (2.0 * math.pi) ** (-0.5)
    return cumulative + pre_act * density


def inner_rows(first, second):
    return lax.dot_general(
        first, second, (((0,), (0,)), ((), ())), preferred_element_type=jnp.float32
    )


def outer_cols(first, second):
    return lax.dot_general(
        first, second, (((1,), (1,)), ((), ())), preferred_element_type=jnp.float32
    )


def clip_forward(block):
    queries, key_rows, value_rows = (block[:, 0], block[:, 1], block[:, 2])
    scores = jnp.einsum(
        "qhd,khd->hqk", queries, key_rows, preferred_element_type=jnp.float32
    ) * HD ** (-0.5)
    row_peak = jnp.max(scores, axis=-1, keepdims=True)
    exponent = jnp.exp(scores - row_peak)
    row_total = jnp.sum(exponent, axis=-1, keepdims=True)
    weights_low = (exponent / row_total).astype(jnp.bfloat16)
    mixed_heads = jnp.einsum(
        "hqk,khd->qhd", weights_low, value_rows, preferred_element_type=jnp.float32
    )
    return (mixed_heads.astype(jnp.bfloat16), (row_peak + jnp.log(row_total))[..., 0])


def clip_backward(element):
    block, grad_mixed, logsum = element
    queries, key_rows, value_rows = (block[:, 0], block[:, 1], block[:, 2])
    scores = jnp.einsum(
        "qhd,khd->hqk", queries, key_rows, preferred_element_type=jnp.float32
    ) * HD ** (-0.5)
    weights_full = jnp.exp(scores - logsum[..., None])
    weights_low = weights_full.astype(jnp.bfloat16)
    grad_values = jnp.einsum(
        "hqk,qhd->khd", weights_low, grad_mixed, preferred_element_type=jnp.float32
    )
    grad_weights = jnp.einsum(
        "qhd,khd->hqk", grad_mixed, value_rows, preferred_element_type=jnp.float32
    )
    row_delta = jnp.sum(grad_weights * weights_full, axis=-1, keepdims=True)
    grad_scores = (weights_full * (grad_weights - row_delta)).astype(jnp.bfloat16)
    grad_queries = jnp.einsum(
        "hqk,khd->qhd", grad_scores, key_rows, preferred_element_type=jnp.float32
    ) * HD ** (-0.5)
    grad_keys = jnp.einsum(
        "hqk,qhd->khd", grad_scores, queries, preferred_element_type=jnp.float32
    ) * HD ** (-0.5)
    return jnp.stack([grad_queries, grad_keys, grad_values], axis=1).astype(jnp.bfloat16)


def per_device(
    tokens,
    w_qkv,
    w_proj,
    w_fc1,
    w_fc2,
    ln1_gain,
    ln1_bias,
    q_bias,
    v_bias,
    proj_bias,
    ln2_gain,
    ln2_bias,
    fc1_bias,
    fc2_bias,
    cotangent,
):
    (
        qkv_part,
        proj_part,
        fc1_part,
        fc2_part,
        gain1_part,
        shift1_part,
        biasq_part,
        biasv_part,
        biasp_part,
        gain2_part,
        shift2_part,
        bias1_part,
        bias2_part,
    ) = (
        lax.all_gather(w_qkv, "row", axis=0, tiled=True),
        lax.all_gather(w_proj, "row", axis=0, tiled=True),
        lax.all_gather(w_fc1, "row", axis=0, tiled=True),
        lax.all_gather(w_fc2, "row", axis=0, tiled=True),
        lax.all_gather(ln1_gain, "row", axis=0, tiled=True),
        lax.all_gather(ln1_bias, "row", axis=0, tiled=True),
        lax.all_gather(q_bias, "row", axis=0, tiled=True),
        lax.all_gather(v_bias, "row", axis=0, tiled=True),
        lax.all_gather(proj_bias, "row", axis=0, tiled=True),
        lax.all_gather(ln2_gain, "row", axis=0, tiled=True),
        lax.all_gather(ln2_bias, "row", axis=0, tiled=True),
        lax.all_gather(fc1_bias, "row", axis=0, tiled=True),
        lax.all_gather(fc2_bias, "row", axis=0, tiled=True),
    )
    (
        full_qkv,
        full_proj,
        full_fc1,
        full_fc2,
        full_gain1,
        full_shift1,
        full_biasq,
        full_biasv,
        full_biasp,
        full_gain2,
        full_shift2,
        full_bias1,
        full_bias2,
    ) = (
        lax.all_gather(qkv_part, "col", axis=1, tiled=True),
        lax.all_gather(proj_part, "col", axis=1, tiled=True),
        lax.all_gather(fc1_part, "col", axis=1, tiled=True),
        lax.all_gather(fc2_part, "col", axis=1, tiled=True),
        lax.all_gather(gain1_part, "col", axis=0, tiled=True),
        lax.all_gather(shift1_part, "col", axis=0, tiled=True),
        lax.all_gather(biasq_part, "col", axis=0, tiled=True),
        lax.all_gather(biasv_part, "col", axis=0, tiled=True),
        lax.all_gather(biasp_part, "col", axis=0, tiled=True),
        lax.all_gather(gain2_part, "col", axis=0, tiled=True),
        lax.all_gather(shift2_part, "col", axis=0, tiled=True),
        lax.all_gather(bias1_part, "col", axis=0, tiled=True),
        lax.all_gather(bias2_part, "col", axis=0, tiled=True),
    )
    gain_first = full_gain1.astype(jnp.float32)
    gain_second = full_gain2.astype(jnp.float32)
    groups = lax.axis_size("row")
    heads_local = H // groups
    per_group = heads_local * HD
    inputs = tokens.astype(jnp.float32)
    token_rows = inputs.shape[0]
    normed_out1, normed_one, inverse_one = layer_norm(
        inputs, gain_first, full_shift1.astype(jnp.float32)
    )
    hidden_one = normed_out1.astype(jnp.bfloat16)
    bias_q = full_biasq.astype(jnp.float32)
    qkv_bias = jnp.concatenate([bias_q, jnp.zeros_like(bias_q), full_biasv.astype(jnp.float32)])
    projected = jnp.dot(hidden_one, full_qkv, preferred_element_type=jnp.float32) + qkv_bias
    qkv_low = projected.astype(jnp.bfloat16).reshape(token_rows, 3, groups, per_group)
    by_heads = lax.all_to_all(qkv_low, "row", split_axis=2, concat_axis=0, tiled=True)
    col_rows = by_heads.shape[0]
    clip_count = col_rows // LEN
    blocks = by_heads.reshape(clip_count, LEN, 3, heads_local, HD)
    mixed_heads, logsum = lax.map(clip_forward, blocks)
    attended = lax.all_to_all(
        mixed_heads.reshape(col_rows, 1, per_group), "row", split_axis=0, concat_axis=1, tiled=True
    ).reshape(token_rows, D)
    middle = inputs + (
        jnp.dot(attended, full_proj, preferred_element_type=jnp.float32)
        + full_biasp.astype(jnp.float32)
    )
    normed_out2, normed_two, inverse_two = layer_norm(
        middle, gain_second, full_shift2.astype(jnp.float32)
    )
    hidden_two = normed_out2.astype(jnp.bfloat16)
    pre_act = jnp.dot(hidden_two, full_fc1, preferred_element_type=jnp.float32) + full_bias1.astype(
        jnp.float32
    )
    activated = jax.nn.gelu(pre_act, approximate=False).astype(jnp.bfloat16)
    result = middle + (
        jnp.dot(activated, full_fc2, preferred_element_type=jnp.float32)
        + full_bias2.astype(jnp.float32)
    )
    qkv_again, proj_again, fc1_again, fc2_again = (
        lax.all_gather(w_qkv, "row", axis=0, tiled=True),
        lax.all_gather(w_proj, "row", axis=0, tiled=True),
        lax.all_gather(w_fc1, "row", axis=0, tiled=True),
        lax.all_gather(w_fc2, "row", axis=0, tiled=True),
    )
    back_qkv, back_proj, back_fc1, back_fc2 = (
        lax.all_gather(qkv_again, "col", axis=1, tiled=True),
        lax.all_gather(proj_again, "col", axis=1, tiled=True),
        lax.all_gather(fc1_again, "col", axis=1, tiled=True),
        lax.all_gather(fc2_again, "col", axis=1, tiled=True),
    )
    grad_out = cotangent.astype(jnp.bfloat16)
    grad_bias2 = jnp.sum(grad_out.astype(jnp.float32), axis=0)
    grad_fc2 = inner_rows(activated, grad_out)
    grad_act = outer_cols(grad_out, back_fc2)
    grad_pre = (grad_act * gelu_slope(pre_act)).astype(jnp.bfloat16)
    grad_bias1 = jnp.sum(grad_pre.astype(jnp.float32), axis=0)
    grad_fc1 = inner_rows(hidden_two, grad_pre)
    grad_hidden2 = outer_cols(grad_pre, back_fc1)
    grad_gain2 = jnp.sum(grad_hidden2 * normed_two, axis=0)
    grad_shift2 = jnp.sum(grad_hidden2, axis=0)
    grad_middle = cotangent + norm_back(grad_hidden2, normed_two, inverse_two, gain_second)
    grad_branch = grad_middle.astype(jnp.bfloat16)
    grad_biasp = jnp.sum(grad_branch.astype(jnp.float32), axis=0)
    grad_proj = inner_rows(attended, grad_branch)
    grad_attended = outer_cols(grad_branch, back_proj).astype(jnp.bfloat16)
    grad_heads = lax.all_to_all(
        grad_attended.reshape(token_rows, groups, per_group),
        "row",
        split_axis=1,
        concat_axis=0,
        tiled=True,
    )
    grad_blocks = grad_heads.reshape(clip_count, LEN, heads_local, HD)
    grad_triple = lax.map(clip_backward, (blocks, grad_blocks, logsum))
    grad_tokens_qkv = lax.all_to_all(
        grad_triple.reshape(col_rows, 3, 1, per_group),
        "row",
        split_axis=0,
        concat_axis=2,
        tiled=True,
    ).reshape(token_rows, 3 * D)
    grad_qkv_float = grad_tokens_qkv.astype(jnp.float32)
    grad_biasq = jnp.sum(grad_qkv_float[:, :D], axis=0)
    grad_biasv = jnp.sum(grad_qkv_float[:, 2 * D :], axis=0)
    grad_qkv = inner_rows(hidden_one, grad_tokens_qkv)
    grad_hidden1 = outer_cols(grad_tokens_qkv, back_qkv)
    grad_gain1 = jnp.sum(grad_hidden1 * normed_one, axis=0)
    grad_shift1 = jnp.sum(grad_hidden1, axis=0)
    grad_inputs = grad_middle + norm_back(grad_hidden1, normed_one, inverse_one, gain_first)
    (
        sum_qkv,
        sum_proj,
        sum_fc1,
        sum_fc2,
        sum_gain1,
        sum_shift1,
        sum_biasq,
        sum_biasv,
        sum_biasp,
        sum_gain2,
        sum_shift2,
        sum_bias1,
        sum_bias2,
    ) = (
        lax.psum_scatter(
            grad_qkv.astype(jnp.bfloat16), "col", scatter_dimension=1, tiled=True
        ).astype(jnp.float32),
        lax.psum_scatter(
            grad_proj.astype(jnp.bfloat16), "col", scatter_dimension=1, tiled=True
        ).astype(jnp.float32),
        lax.psum_scatter(
            grad_fc1.astype(jnp.bfloat16), "col", scatter_dimension=1, tiled=True
        ).astype(jnp.float32),
        lax.psum_scatter(
            grad_fc2.astype(jnp.bfloat16), "col", scatter_dimension=1, tiled=True
        ).astype(jnp.float32),
        lax.psum_scatter(
            grad_gain1.astype(jnp.bfloat16), "col", scatter_dimension=0, tiled=True
        ).astype(jnp.float32),
        lax.psum_scatter(
            grad_shift1.astype(jnp.bfloat16), "col", scatter_dimension=0, tiled=True
        ).astype(jnp.float32),
        lax.psum_scatter(
            grad_biasq.astype(jnp.bfloat16), "col", scatter_dimension=0, tiled=True
        ).astype(jnp.float32),
        lax.psum_scatter(
            grad_biasv.astype(jnp.bfloat16), "col", scatter_dimension=0, tiled=True
        ).astype(jnp.float32),
        lax.psum_scatter(
            grad_biasp.astype(jnp.bfloat16), "col", scatter_dimension=0, tiled=True
        ).astype(jnp.float32),
        lax.psum_scatter(
            grad_gain2.astype(jnp.bfloat16), "col", scatter_dimension=0, tiled=True
        ).astype(jnp.float32),
        lax.psum_scatter(
            grad_shift2.astype(jnp.bfloat16), "col", scatter_dimension=0, tiled=True
        ).astype(jnp.float32),
        lax.psum_scatter(
            grad_bias1.astype(jnp.bfloat16), "col", scatter_dimension=0, tiled=True
        ).astype(jnp.float32),
        lax.psum_scatter(
            grad_bias2.astype(jnp.bfloat16), "col", scatter_dimension=0, tiled=True
        ).astype(jnp.float32),
    )
    (
        out_qkv,
        out_proj,
        out_fc1,
        out_fc2,
        out_gain1,
        out_shift1,
        out_biasq,
        out_biasv,
        out_biasp,
        out_gain2,
        out_shift2,
        out_bias1,
        out_bias2,
    ) = (
        lax.psum_scatter(
            sum_qkv.astype(jnp.bfloat16), "row", scatter_dimension=0, tiled=True
        ).astype(jnp.float32),
        lax.psum_scatter(
            sum_proj.astype(jnp.bfloat16), "row", scatter_dimension=0, tiled=True
        ).astype(jnp.float32),
        lax.psum_scatter(
            sum_fc1.astype(jnp.bfloat16), "row", scatter_dimension=0, tiled=True
        ).astype(jnp.float32),
        lax.psum_scatter(
            sum_fc2.astype(jnp.bfloat16), "row", scatter_dimension=0, tiled=True
        ).astype(jnp.float32),
        lax.psum_scatter(
            sum_gain1.astype(jnp.bfloat16), "row", scatter_dimension=0, tiled=True
        ).astype(jnp.float32),
        lax.psum_scatter(
            sum_shift1.astype(jnp.bfloat16), "row", scatter_dimension=0, tiled=True
        ).astype(jnp.float32),
        lax.psum_scatter(
            sum_biasq.astype(jnp.bfloat16), "row", scatter_dimension=0, tiled=True
        ).astype(jnp.float32),
        lax.psum_scatter(
            sum_biasv.astype(jnp.bfloat16), "row", scatter_dimension=0, tiled=True
        ).astype(jnp.float32),
        lax.psum_scatter(
            sum_biasp.astype(jnp.bfloat16), "row", scatter_dimension=0, tiled=True
        ).astype(jnp.float32),
        lax.psum_scatter(
            sum_gain2.astype(jnp.bfloat16), "row", scatter_dimension=0, tiled=True
        ).astype(jnp.float32),
        lax.psum_scatter(
            sum_shift2.astype(jnp.bfloat16), "row", scatter_dimension=0, tiled=True
        ).astype(jnp.float32),
        lax.psum_scatter(
            sum_bias1.astype(jnp.bfloat16), "row", scatter_dimension=0, tiled=True
        ).astype(jnp.float32),
        lax.psum_scatter(
            sum_bias2.astype(jnp.bfloat16), "row", scatter_dimension=0, tiled=True
        ).astype(jnp.float32),
    )
    return (
        result.astype(jnp.bfloat16),
        grad_inputs,
        out_qkv,
        out_proj,
        out_fc1,
        out_fc2,
        out_gain1,
        out_shift1,
        out_biasq,
        out_biasv,
        out_biasp,
        out_gain2,
        out_shift2,
        out_bias1,
        out_bias2,
    )


def solution(mesh):
    return jax.shard_map(
        per_device,
        mesh=mesh,
        in_specs=(
            P(("col", "row"), None),
            P("row", "col"),
            P("row", "col"),
            P("row", "col"),
            P("row", "col"),
            P(("col", "row")),
            P(("col", "row")),
            P(("col", "row")),
            P(("col", "row")),
            P(("col", "row")),
            P(("col", "row")),
            P(("col", "row")),
            P(("col", "row")),
            P(("col", "row")),
            P(("col", "row"), None),
        ),
        out_specs=(
            P(("col", "row"), None),
            P(("col", "row"), None),
            P("row", "col"),
            P("row", "col"),
            P("row", "col"),
            P("row", "col"),
            P(("col", "row")),
            P(("col", "row")),
            P(("col", "row")),
            P(("col", "row")),
            P(("col", "row")),
            P(("col", "row")),
            P(("col", "row")),
            P(("col", "row")),
            P(("col", "row")),
        ),
        check_vma=False,
    )
```

profile of v0, /device:TPU:0, one launch (start us, length us, event | category | flops | bytes accessed | tf_op | source)
XLA Modules:
  0.0 1200.0 jit_solution(12227109749676747950)
XLA Ops:
  48.5 59.9 %all-reduce.35 = (bf16[1024]{0:T(1024)(128)(2,1)S(1)}, bf16[1024]{0:T(1024)(128)(2,1)S(1)}, bf16[1024]{0:T(1024)(128)(2,1)S(1)}, bf16[1024]{0:T(1024)(128)(2,1)S...) all-reduce(bf16[1024]{0:T(1024)(128)(2,1)S(1)} %dynamic-update-slic, ...), channel_id=1, replica_groups=mesh['row'=2,'col'=16] {'col'}, use_global_device_ids=true, to_apply=%add.7 | all-reduce | flops 7168 | bytes 28672
  144.3 55.4 %all_gather.108 = bf16[4096,64]{0,1:T(8,128)(2,1)} all-gather(bf16[2048,64]{0,1:T(8,128)(2,1)S(1)} %copy-done.11), channel_id=1, replica_groups=mesh['row'=2,'col'=16] {'row'}, dimensions={0}, use_global_device_ids=true | all-gather | bytes 786432 | tf_op jit(solution)/shard_map/all_gather | solution.py:123
  225.7 32.2 %multiply_reduce_fusion.1 = (f32[8,1568]{1,0:T(8,128)S(1)}, f32[8,1568,1568]{1,2,0:T(8,128)}) fusion(bf16[1568,3,8,64]{0,3,2,1:T(8,128)(2,1)} %squeeze.35), kind=kOutput, calls=%fused_computation.6 | convolution fusion | flops 2556956416 | bytes 82134016 | tf_op jit(solution)/shard_map/while/body/eval_jaxpr/qhd,khd->hqk/dot_general | solution.py:50
  257.9 26.7 %fusion = f32[8,1568]{1,0:T(8,128)S(1)} fusion(f32[8,1568,1568]{1,2,0:T(8,128)} %get-tuple-element.94, f32[8,1568]{1,0:T(8,128)S(1)} %get-tuple-element.93), kind=kLoop, calls=%fused_computation.5 | loop fusion | flops 58994432 | bytes 78776320 | tf_op jit(solution)/shard_map/while/body/eval_jaxpr/reduce_sum | solution.py:55
  284.7 30.8 %fusion.38 = bf16[8,64,1568]{2,1,0:T(8,128)(2,1)S(1)} fusion(f32[8,1568,1568]{1,2,0:T(8,128)} %get-tuple-element.94, f32[8,1568]{1,0:T(8,128)S(1)} %fusion, f32[8,1568]{1,0:T(8,128)S(1)} %get-tuple-element.93, bf16[1568,3,8,64]{0,3,2,1:T(8,128)(2,1)} %squeeze.35), kind=kOutput, calls=%fused_computation.70 | convolution fusion | flops 2597109760 | bytes 86902784 | tf_op jit(solution)/shard_map/while/body/eval_jaxpr/hqk,khd->qhd/dot_general | solution.py:57
  325.2 14.5 %all-gather = bf16[2,1,128]{2,1,0:T(2,128)(2,1)S(1)} all-gather(bf16[1,1,128]{2,1,0:T(2,128)(2,1)S(1)} %bitcast.100), channel_id=1, replica_groups=mesh['row'=2,'col'=16] {'row'}, dimensions={0}, use_global_device_ids=true | all-gather | bytes 768 | tf_op jit(solution)/shard_map/all_gather | solution.py:131
  339.7 25.8 %all-gather.1 = bf16[16,1,256]{2,1,0:T(2,128)(2,1)S(1)} all-gather(bf16[1,1,256]{2,1,0:T(2,128)(2,1)S(1)} %bitcast.99), channel_id=1, replica_groups=mesh['row'=2,'col'=16] {'col'}, dimensions={0}, use_global_device_ids=true | all-gather | bytes 8704 | tf_op jit(solution)/shard_map/all_gather | solution.py:160
  379.1 39.0 %fusion.7 = (bf16[784,4096]{1,0:T(8,128)(2,1)}, f32[784,4096]{1,0:T(8,128)}) fusion(f32[4096]{0:T(1024)S(1)} %bitcast.97, bf16[1024,4096]{1,0:T(8,128)(2,1)} %all-gather.11.cloned.1.call-done, f32[784,1024]{1,0:T(8,128)} %copy-done.5, f32[1024]{0:T(1024)S(1)} %convert_element_type.201, f32[1024]{0:T(1024)S(1)} %convert_element_type.200, ...), kind=kOutput, calls=%fused_computation.14 | convolution fusion | flops 6792626176 | bytes 30898304 | tf_op jit(solution)/shard_map/dot_general | solution.py:194
  418.1 17.1 %fusion.53 = (bf16[4096]{0:T(1024)(128)(2,1)}, bf16[784,4096]{1,0:T(8,128)(2,1)}) fusion(f32[784,4096]{1,0:T(8,128)} %get-tuple-element.104, f32[4096]{0:T(1024)S(1)} %bitcast.98, bf16[4096,1024]{0,1:T(8,128)(2,1)} %all-gather.13.cloned.1.call-done, f32[784,1024]{1,0:T(8,128)S(1)} %copy-done.7), kind=kOutput, calls=%fused_computation.112 | convolution fusion | flops 6616002560 | bytes 30892032 | tf_op jit(solution)/shard_map/dot_general | solution.py:43
  455.1 20.3 %all-to-all-done.2 = bf16[784,2,512]{2,0,1:T(8,128)(2,1)S(1)} async-done(((bf16[784,2,512]{2,0,1:T(8,128)(2,1)}), bf16[784,2,512]{2,0,1:T(8,128)(2,1)S(1)}, u32[]{:S(2)}, u32[]{:S(2)}) %all-to-all-start.2) | async-done | bytes 1605664 | tf_op jit(solution)/shard_map/all_to_all | solution.py:229
  483.4 29.4 %fusion.35 = bf16[8,64,1568]{2,1,0:T(8,128)(2,1)} fusion(bf16[1568,8,64]{0,2,1:T(8,128)(2,1)S(1)} %squeeze.39, f32[8,1568,1568]{1,2,0:T(8,128)} %get-tuple-element.94, f32[8,1568]{1,0:T(8,128)S(1)} %log_add_fusion), kind=kOutput, calls=%fused_computation.69 | convolution fusion | flops 2577440768 | bytes 81937408 | tf_op jit(solution)/shard_map/while/body/eval_jaxpr/hqk,qhd->khd/dot_general | solution.py:71
  512.9 56.6 %multiply_reduce_fusion = (f32[8,1568]{1,0:T(8,128)S(1)}, f32[8,1568,1568]{1,2,0:T(8,128)}) fusion(f32[8,1568,1568]{1,2,0:T(8,128)} %get-tuple-element.94, f32[8,1568]{1,0:T(8,128)S(1)} %log_add_fusion, bf16[1568,8,64]{0,2,1:T(8,128)(2,1)S(1)} %squeeze.39, bf16[1568,3,8,64]{0,3,2,1:T(8,128)(2,1)} %squeeze.35), kind=kOutput, calls=%fused_computation.1 | convolution fusion | flops 2596294400 | bytes 165578752 | tf_op jit(solution)/shard_map/while/body/eval_jaxpr/qhd,khd->hqk/dot_general | solution.py:74
  569.5 64.8 %multiply_convert_fusion = bf16[8,1568,1568]{1,2,0:T(8,128)(2,1)} fusion(f32[8,1568,1568]{1,2,0:T(8,128)} %get-tuple-element.99, f32[8,1568,1568]{1,2,0:T(8,128)} %get-tuple-element.94, f32[8,1568]{1,0:T(8,128)S(1)} %get-tuple-element.98, f32[8,1568]{1,0:T(8,128)S(1)} %log_add_fusion), kind=kLoop, calls=%fused_computation | loop fusion | flops 98344960 | bytes 196790272 | tf_op jit(solution)/shard_map/while/body/eval_jaxpr/convert_element_type | solution.py:78
  634.3 20.6 %multiply_convert_fusion.1 = bf16[8,64,1568]{2,1,0:T(8,128)(2,1)} fusion(bf16[8,1568,1568]{1,2,0:T(8,128)(2,1)} %multiply_convert_fusion, bf16[1568,3,8,64]{0,3,2,1:T(8,128)(2,1)} %squeeze.35), kind=kOutput, calls=%fused_computation.50 | convolution fusion | flops 2519236608 | bytes 45056000 | tf_op jit(solution)/shard_map/while/body/eval_jaxpr/hqk,qhd->khd/dot_general | solution.py:82
  654.9 21.0 %multiply_convert_fusion.2 = bf16[8,64,1568]{2,1,0:T(8,128)(2,1)} fusion(bf16[8,1568,1568]{1,2,0:T(8,128)(2,1)} %multiply_convert_fusion, bf16[1568,3,8,64]{0,3,2,1:T(8,128)(2,1)} %squeeze.35), kind=kOutput, calls=%fused_computation.51 | convolution fusion | flops 2519236608 | bytes 45056000 | tf_op jit(solution)/shard_map/while/body/eval_jaxpr/hqk,khd->qhd/dot_general | solution.py:79
  728.4 65.8 %all-to-all-done.3 = bf16[1568,3,1,512]{3,1,2,0:T(4,128)(2,1)} async-done(((bf16[1568,3,1,512]{3,1,2,0:T(4,128)(2,1)}), bf16[1568,3,1,512]{3,1,2,0:T(4,128)(2,1)}, u32[]{:S(2)}, u32[]{:S(2)}) %all-to-all-start.3) | async-done | bytes 4816928 | tf_op jit(solution)/shard_map/all_to_all | solution.py:238
  834.3 15.0 %convolution_convert_fusion.1 = bf16[1024,4096]{1,0:T(8,128)(2,1)} fusion(bf16[784,4096]{1,0:T(8,128)(2,1)} %get-tuple-element.102, f32[784,1024]{1,0:T(8,128)} %copy-done.5, f32[1024]{0:T(1024)S(1)} %copy-done.32, f32[1024]{0:T(1024)S(1)} %copy-done.23, f32[784]{0:T(1024)S(1)} %copy-done.25, f32[784]{0:T(1024)S(1)} %copy-done.17), kind=kOutput, calls=%fused_computation.38 | convolution fusion | flops 6584877056 | bytes 18036864 | tf_op jit(solution)/shard_map/dot_general | solution.py:37
  849.3 14.9 %convolution_convert_fusion = bf16[4096,1024]{0,1:T(8,128)(2,1)} fusion(bf16[784,4096]{1,0:T(8,128)(2,1)} %get-tuple-element.103, f32[784,1024]{1,0:T(8,128)} %param.29), kind=kOutput, calls=%fused_computation.37 | convolution fusion | flops 6581665792 | bytes 18022400 | tf_op jit(solution)/shard_map/dot_general | solution.py:37
  867.9 47.0 %reduce-scatter.9.cloned.1.call-done = bf16[1024,192]{0,1:T(8,128)(2,1)} async-done(((bf16[1024,3072]{0,1:T(8,128)(2,1)}), bf16[1024,192]{0,1:T(8,128)(2,1)}) %reduce-scatter.9.cloned.1.call-update) | async-done | bytes 393232 | tf_op jit(solution)/shard_map/reduce_scatter | solution.py:268
  930.3 61.4 %all-reduce.34 = (bf16[1024]{0:T(1024)(128)(2,1)S(1)}, bf16[1024]{0:T(1024)(128)(2,1)S(1)}, bf16[1024]{0:T(1024)(128)(2,1)S(1)}, bf16[1024]{0:T(1024)(128)(2,1)S...) all-reduce(bf16[1024]{0:T(1024)(128)(2,1)S(1)} %dynamic-update-slic, ...), channel_id=1, replica_groups=mesh['row'=2,'col'=16] {'col'}, use_global_device_ids=true, to_apply=%add.15 | all-reduce | flops 13312 | bytes 53248
  991.7 30.7 %reduce-scatter.17.cloned.1.call-done = bf16[1024,256]{1,0:T(8,128)(2,1)} async-done(((bf16[1024,4096]{1,0:T(8,128)(2,1)}), bf16[1024,256]{1,0:T(8,128)(2,1)}) %reduce-scatter.17.cloned.1.call-update) | async-done | bytes 524304 | tf_op jit(solution)/shard_map/reduce_scatter | solution.py:274
  1045.3 84.3 %reduce-scatter.21.cloned.1.call-done = bf16[4096,64]{0,1:T(8,128)(2,1)} async-done(((bf16[4096,1024]{0,1:T(8,128)(2,1)}), bf16[4096,64]{0,1:T(8,128)(2,1)}) %reduce-scatter.21.cloned.1.call-update) | async-done | bytes 524304 | tf_op jit(solution)/shard_map/reduce_scatter | solution.py:277
  1158.9 15.2 %reduce-scatter.19.cloned.1.call-done = bf16[512,256]{1,0:T(8,128)(2,1)} async-done(((bf16[1024,256]{1,0:T(8,128)(2,1)}), bf16[512,256]{1,0:T(8,128)(2,1)}) %reduce-scatter.19.cloned.1.call-update) | async-done | bytes 262160 | tf_op jit(solution)/shard_map/reduce_scatter | solution.py:329
  1175.9 15.0 %reduce-scatter.23.cloned.1.call-done = bf16[2048,64]{0,1:T(8,128)(2,1)} async-done(((bf16[4096,64]{0,1:T(8,128)(2,1)}), bf16[2048,64]{0,1:T(8,128)(2,1)}) %reduce-scatter.23.cloned.1.call-update) | async-done | bytes 262160 | tf_op jit(solution)/shard_map/reduce_scatter | solution.py:332
  (238 shorter events, 317.3 us)
Async XLA Ops:
  7.2 102.9 %copy-start = (bf16[784,1024]{1,0:T(8,128)(2,1)S(1)}, bf16[784,1024]{1,0:T(8,128)(2,1)}, u32[]{:S(2)}) copy-start(bf16[784,1024]{1,0:T(8,128)(2,1)} %param.15) | copy-start | bytes 4816900
  7.2 103.6 %all-gather.7.cloned.1.call-start = ((), (), s32[]{:S(2)}) async-start(), calls=%async_computation.12 | async-start | bytes 6684672 | tf_op jit(solution)/shard_map/all_gather | solution.py:149
  17.9 354.8 %all-gather.9.cloned.1.call-start = ((), (), s32[]{:S(2)}) async-start(), calls=%async_computation.13 | async-start | bytes 2228224 | tf_op jit(solution)/shard_map/all_gather | solution.py:150
  23.2 355.8 %all-gather.11.cloned.1.call-start = ((), (), s32[]{:S(2)}) async-start(), calls=%async_computation.14 | async-start | bytes 8912896 | tf_op jit(solution)/shard_map/all_gather | solution.py:151
  138.3 61.4 %all-to-all-start = ((bf16[784,3,2,512]{3,0,1,2:T(8,128)(2,1)}), bf16[784,3,2,512]{3,0,1,2:T(8,128)(2,1)}, u32[]{:S(2)}, u32[]{:S(2)}) async-start(bf16[784,3,2,512]{3,0,1,2:T(8,128)(2,1)} %copy.48), calls=%async_computation | async-start | bytes 9633792 | tf_op jit(solution)/shard_map/all_to_all | solution.py:178
  144.3 273.8 %all-gather.13.cloned.1.call-start = ((), (), s32[]{:S(2)}) async-start(), calls=%async_computation.15 | async-start | bytes 8912896 | tf_op jit(solution)/shard_map/all_gather | solution.py:152
  257.9 26.7 %copy-start.9 = (f32[8,1568]{1,0:T(8,128)}, f32[8,1568]{1,0:T(8,128)S(1)}, u32[]{:S(2)}) copy-start(f32[8,1568]{1,0:T(8,128)S(1)} %get-tuple-element.93) | copy-start | bytes 150532
  284.7 30.8 %copy-start.12 = (f32[8,1568]{1,0:T(8,128)}, f32[8,1568]{1,0:T(8,128)S(1)}, u32[]{:S(2)}) copy-start(f32[8,1568]{1,0:T(8,128)S(1)} %fusion) | copy-start | bytes 150532
  321.5 44.1 %all-to-all-start.1 = ((bf16[2,2,200704]{2,1,0:T(2,128)(2,1)}), bf16[2,2,200704]{2,1,0:T(2,128)(2,1)S(1)}, u32[]{:S(2)}, u32[]{:S(2)}) async-start(bf16[2,2,200704]{2,1,0:T(2,128)(2,1)} %reshape.277), calls=%async_computation.1 | async-start | bytes 3211264 | tf_op jit(solution)/shard_map/all_to_all | solution.py:183
  325.2 121.1 %copy-start.22 = (f32[1024]{0:T(1024)}, f32[1024]{0:T(1024)S(1)}, u32[]{:S(2)}) copy-start(f32[1024]{0:T(1024)S(1)} %convert_element_type.200) | copy-start | bytes 12292
  325.2 53.9 %copy-start.31 = (f32[1024]{0:T(1024)}, f32[1024]{0:T(1024)S(1)}, u32[]{:S(2)}) copy-start(f32[1024]{0:T(1024)S(1)} %convert_element_type.201) | copy-start | bytes 12292
  376.9 69.4 %copy-start.16 = (f32[784]{0:T(1024)}, f32[784]{0:T(1024)S(1)}, u32[]{:S(2)}) copy-start(f32[784]{0:T(1024)S(1)} %broadcast_multiply_fusion.4) | copy-start | bytes 9412
  379.0 67.2 %copy-start.24 = (f32[784]{0:T(1024)}, f32[784]{0:T(1024)S(1)}, u32[]{:S(2)}) copy-start(f32[784]{0:T(1024)S(1)} %add_rsqrt_fusion) | copy-start | bytes 9412
  379.1 39.0 %copy-start.7 = (f32[784,1024]{1,0:T(8,128)S(1)}, f32[784,1024]{1,0:T(8,128)}, u32[]{:S(2)}) copy-start(f32[784,1024]{1,0:T(8,128)} %param.29) | copy-start | bytes 9633796
  451.4 24.0 %all-to-all-start.2 = ((bf16[784,2,512]{2,0,1:T(8,128)(2,1)}), bf16[784,2,512]{2,0,1:T(8,128)(2,1)S(1)}, u32[]{:S(2)}, u32[]{:S(2)}) async-start(bf16[784,2,512]{2,0,1:T(8,128)(2,1)} %bitcast.85), calls=%async_computation.2 | async-start | bytes 3211264 | tf_op jit(solution)/shard_map/all_to_all | solution.py:229
  716.4 77.9 %all-to-all-start.3 = ((bf16[1568,3,1,512]{3,1,2,0:T(4,128)(2,1)}), bf16[1568,3,1,512]{3,1,2,0:T(4,128)(2,1)}, u32[]{:S(2)}, u32[]{:S(2)}) async-start(bf16[1568,3,1,512]{3,1,2,0:T(4,128)(2,1)} %pad_maximum_fusion), calls=%async_computation.3 | async-start | bytes 12845056 | tf_op jit(solution)/shard_map/all_to_all | solution.py:238
  723.0 141.3 %reduce-scatter.13.cloned.1.call-start = ((), (), s32[]{:S(2)}) async-start(), calls=%async_computation.18 | async-start | bytes 2228224 | tf_op jit(solution)/shard_map/reduce_scatter | solution.py:271
  728.2 186.7 %reduce-scatter.9.cloned.1.call-start = ((), (), s32[]{:S(2)}) async-start(), calls=%async_computation.16 | async-start | bytes 6684672 | tf_op jit(solution)/shard_map/reduce_scatter | solution.py:268
  833.6 188.8 %reduce-scatter.17.cloned.1.call-start = ((), (), s32[]{:S(2)}) async-start(), calls=%async_computation.20 | async-start | bytes 8912896 | tf_op jit(solution)/shard_map/reduce_scatter | solution.py:274
  849.3 280.4 %reduce-scatter.21.cloned.1.call-start = ((), (), s32[]{:S(2)}) async-start(), calls=%async_computation.22 | async-start | bytes 8912896 | tf_op jit(solution)/shard_map/reduce_scatter | solution.py:277
  864.3 277.6 %reduce-scatter.15.cloned.1.call-start = ((), (), s32[]{:S(2)}) async-start(), calls=%async_computation.19 | async-start | bytes 196608 | tf_op jit(solution)/shard_map/reduce_scatter | solution.py:326
  865.0 292.2 %reduce-scatter.11.cloned.1.call-start = ((), (), s32[]{:S(2)}) async-start(), calls=%async_computation.17 | async-start | bytes 589824 | tf_op jit(solution)/shard_map/reduce_scatter | solution.py:323
  914.9 259.2 %reduce-scatter.19.cloned.1.call-start = ((), (), s32[]{:S(2)}) async-start(), calls=%async_computation.21 | async-start | bytes 786432 | tf_op jit(solution)/shard_map/reduce_scatter | solution.py:329
  1022.4 168.5 %reduce-scatter.23.cloned.1.call-start = ((), (), s32[]{:S(2)}) async-start(), calls=%async_computation.23 | async-start | bytes 786432 | tf_op jit(solution)/shard_map/reduce_scatter | solution.py:332
  (34 other events, 216.9 us)
Sparse Core Ops, SparseCore 0:
  18.0 62.1 all-gather.6
  82.3 40.4 all-gather.8
  125.0 76.2 all-gather.10
  203.3 72.4 all-gather.12
  728.3 59.4 reduce-scatter.12
  833.7 81.1 reduce-scatter.8
  919.0 103.3 reduce-scatter.16
  1026.5 103.1 reduce-scatter.20
  1131.8 10.0 reduce-scatter.14
  1144.0 13.1 reduce-scatter.10
  1159.5 14.6 reduce-scatter.18
  1176.2 14.6 reduce-scatter.22
where the time goes:
time: 1210 us; the launch traced here: 1200 us
  matrix products  343 us (28%)
  waiting for transfers between devices  300 us (25%)
  blocking collectives  252 us (21%)
  other arithmetic  133 us (11%)
  local copies, waits for them, and re-layouts  131 us (11%)
  starting transfers between devices  20.7 us (2%)
  between operations  19.3 us (2%)
    unnamed x4, blocking collectives  132 us
    reduce_scatter x1, waiting for transfers between devices, per_device(): lax.psum_scatter(grad_fc2.astype(jnp.bfloat16), 'col', scatter_dimension=...  84.3 us
    all_to_all x1, waiting for transfers between devices, per_device(): lax.all_to_all(grad_triple.reshape(col_rows, 3, 1, per_group), 'row', spl...  65.8 us
    convert_element_type x1, other arithmetic, clip_backward(): (weights_full * (grad_weights - row_delta)).astype(jnp.bfloat16)  64.8 us
    dot_general x1, matrix products, clip_backward(): jnp.einsum('qhd,khd->hqk', grad_mixed, value_rows, preferred_element_type...  56.6 us
    all_gather x1, blocking collectives, per_device(): lax.all_gather(w_fc2, 'row', axis=0, tiled=True)  55.4 us
    reduce_scatter x1, waiting for transfers between devices, per_device(): lax.psum_scatter(grad_qkv.astype(jnp.bfloat16), 'col', scatter_dimension=...  47 us
    dot_general x4, matrix products, inner_rows(): lax.dot_general(first, second, (((0,), (0,)), ((), ())), preferred_elemen...  46.4 us
  transfers between devices with their start and end apart: 16, of which 9 were waited for; matrix products, arithmetic and copies ran while one was open for 27% of the time, Pallas kernels for 0%

commit v1 on v0

--- a/solution.py
+++ b/solution.py
@@ -235,12 +235,18 @@
     )
     grad_blocks = grad_heads.reshape(clip_count, LEN, heads_local, HD)
     grad_triple = lax.map(clip_backward, (blocks, grad_blocks, logsum))
-    grad_tokens_qkv = lax.all_to_all(
-        grad_triple.reshape(col_rows, 3, 1, per_group),
-        "row",
-        split_axis=0,
-        concat_axis=2,
-        tiled=True,
+    grad_tokens_qkv = jnp.concatenate(
+        lax.all_to_all(
+            jnp.stack(
+                jnp.split(
+                    grad_triple.reshape(col_rows, 3, 1, per_group), lax.axis_size("row"), axis=0
+                )
+            ),
+            "row",
+            0,
+            0,
+        ),
+        axis=2,
     ).reshape(token_rows, 3 * D)
     grad_qkv_float = grad_tokens_qkv.astype(jnp.float32)
     grad_biasq = jnp.sum(grad_qkv_float[:, :D], axis=0)

time: 1210 us -> 1160 us (0.959)
  local copies, waits for them, and re-layouts: 131 us -> 108 us
  waiting for transfers between devices: 300 us -> 282 us
    all_to_all x1, waiting for transfers between devices: 65.8 us -> 48.5 us  [per_device(): lax.all_to_all(jnp.stack(jnp.split(grad_triple.reshape(col_rows, 3, 1, pe...]
    all_to_all x2 -> x0, local copies, waits for them, and re-layouts: 15.8 us -> none  [per_device(): lax.all_to_all(grad_triple.reshape(col_rows, 3, 1, per_group), 'row', spl...]
  transfers between devices with their start and end apart: 16 -> 16, of which waited for: 9 -> 9; matrix products, arithmetic and copies ran while one was open for 27% -> 28% of each run, Pallas kernels for 0% -> 0%
where the time goes in v1:
time: 1160 us; the launch traced here: 1150 us
  matrix products  341 us (29%)
  waiting for transfers between devices  282 us (24%)
  blocking collectives  251 us (22%)
  other arithmetic  127 us (11%)
  local copies, waits for them, and re-layouts  108 us (9%)
  starting transfers between devices  20.7 us (2%)
  between operations  19 us (2%)
    unnamed x4, blocking collectives  132 us
    reduce_scatter x1, waiting for transfers between devices, per_device(): lax.psum_scatter(grad_fc2.astype(jnp.bfloat16), 'col', scatter_dimension=...  84.3 us
    convert_element_type x1, other arithmetic, clip_backward(): (weights_full * (grad_weights - row_delta)).astype(jnp.bfloat16)  64.7 us
    dot_general x1, matrix products, clip_backward(): jnp.einsum('qhd,khd->hqk', grad_mixed, value_rows, preferred_element_type...  56.5 us
    all_gather x1, blocking collectives, per_device(): lax.all_gather(w_fc2, 'row', axis=0, tiled=True)  55.4 us
    all_to_all x1, waiting for transfers between devices, per_device(): lax.all_to_all(jnp.stack(jnp.split(grad_triple.reshape(col_rows, 3, 1, pe...  48.5 us
    reduce_scatter x1, waiting for transfers between devices, per_device(): lax.psum_scatter(grad_qkv.astype(jnp.bfloat16), 'col', scatter_dimension=...  47.1 us
    dot_general x4, matrix products, inner_rows(): lax.dot_general(first, second, (((0,), (0,)), ((), ())), preferred_elemen...  46.3 us
  transfers between devices with their start and end apart: 16, of which 9 were waited for; matrix products, arithmetic and copies ran while one was open for 28% of the time, Pallas kernels for 0%

profile of v1, /device:TPU:0, one launch (start us, length us, event | category | flops | bytes accessed | tf_op | source)
XLA Modules:
  0.0 1149.1 jit_solution(12243304847570573564)
XLA Ops:
  48.5 59.8 %all-reduce.35 = (bf16[1024]{0:T(1024)(128)(2,1)S(1)}, bf16[1024]{0:T(1024)(128)(2,1)S(1)}, bf16[1024]{0:T(1024)(128)(2,1)S(1)}, bf16[1024]{0:T(1024)(128)(2,1)S...) all-reduce(bf16[1024]{0:T(1024)(128)(2,1)S(1)} %dynamic-update-slic, ...), channel_id=1, replica_groups=mesh['row'=2,'col'=16] {'col'}, use_global_device_ids=true, to_apply=%add.7 | all-reduce | flops 7168 | bytes 28672
  144.4 55.4 %all_gather.108 = bf16[4096,64]{0,1:T(8,128)(2,1)} all-gather(bf16[2048,64]{0,1:T(8,128)(2,1)S(1)} %copy-done.11), channel_id=1, replica_groups=mesh['row'=2,'col'=16] {'row'}, dimensions={0}, use_global_device_ids=true | all-gather | bytes 786432 | tf_op jit(solution)/shard_map/all_gather | solution.py:123
  225.8 32.2 %multiply_reduce_fusion.1 = (f32[8,1568]{1,0:T(8,128)S(1)}, f32[8,1568,1568]{1,2,0:T(8,128)}) fusion(bf16[1568,3,8,64]{0,3,2,1:T(8,128)(2,1)} %squeeze.35), kind=kOutput, calls=%fused_computation.6 | convolution fusion | flops 2556956416 | bytes 82134016 | tf_op jit(solution)/shard_map/while/body/eval_jaxpr/qhd,khd->hqk/dot_general | solution.py:50
  258.0 26.7 %fusion = f32[8,1568]{1,0:T(8,128)S(1)} fusion(f32[8,1568,1568]{1,2,0:T(8,128)} %get-tuple-element.96, f32[8,1568]{1,0:T(8,128)S(1)} %get-tuple-element.95), kind=kLoop, calls=%fused_computation.5 | loop fusion | flops 58994432 | bytes 78776320 | tf_op jit(solution)/shard_map/while/body/eval_jaxpr/reduce_sum | solution.py:55
  284.8 30.6 %fusion.38 = bf16[8,64,1568]{2,1,0:T(8,128)(2,1)S(1)} fusion(f32[8,1568,1568]{1,2,0:T(8,128)} %get-tuple-element.96, f32[8,1568]{1,0:T(8,128)S(1)} %fusion, f32[8,1568]{1,0:T(8,128)S(1)} %get-tuple-element.95, bf16[1568,3,8,64]{0,3,2,1:T(8,128)(2,1)} %squeeze.35), kind=kOutput, calls=%fused_computation.71 | convolution fusion | flops 2597109760 | bytes 86902784 | tf_op jit(solution)/shard_map/while/body/eval_jaxpr/hqk,khd->qhd/dot_general | solution.py:57
  325.1 14.4 %all-gather = bf16[2,1,128]{2,1,0:T(2,128)(2,1)S(1)} all-gather(bf16[1,1,128]{2,1,0:T(2,128)(2,1)S(1)} %bitcast.101), channel_id=1, replica_groups=mesh['row'=2,'col'=16] {'row'}, dimensions={0}, use_global_device_ids=true | all-gather | bytes 768 | tf_op jit(solution)/shard_map/all_gather | solution.py:131
  339.6 25.1 %all-gather.1 = bf16[16,1,256]{2,1,0:T(2,128)(2,1)S(1)} all-gather(bf16[1,1,256]{2,1,0:T(2,128)(2,1)S(1)} %bitcast.100), channel_id=1, replica_groups=mesh['row'=2,'col'=16] {'col'}, dimensions={0}, use_global_device_ids=true | all-gather | bytes 8704 | tf_op jit(solution)/shard_map/all_gather | solution.py:160
  378.2 39.0 %fusion.7 = (bf16[784,4096]{1,0:T(8,128)(2,1)}, f32[784,4096]{1,0:T(8,128)}) fusion(f32[4096]{0:T(1024)S(1)} %bitcast.98, bf16[1024,4096]{1,0:T(8,128)(2,1)} %all-gather.11.cloned.1.call-done, f32[784,1024]{1,0:T(8,128)} %copy-done.5, f32[1024]{0:T(1024)S(1)} %convert_element_type.194, f32[1024]{0:T(1024)S(1)} %convert_element_type.193, ...), kind=kOutput, calls=%fused_computation.14 | convolution fusion | flops 6792626176 | bytes 30898304 | tf_op jit(solution)/shard_map/dot_general | solution.py:194
  417.3 17.2 %fusion.59 = (bf16[4096]{0:T(1024)(128)(2,1)}, bf16[784,4096]{1,0:T(8,128)(2,1)}) fusion(f32[784,4096]{1,0:T(8,128)} %get-tuple-element.106, f32[4096]{0:T(1024)S(1)} %bitcast.99, bf16[4096,1024]{0,1:T(8,128)(2,1)} %all-gather.13.cloned.1.call-done, f32[784,1024]{1,0:T(8,128)S(1)} %copy-done.7), kind=kOutput, calls=%fused_computation.117 | convolution fusion | flops 6616002560 | bytes 30892032 | tf_op jit(solution)/shard_map/dot_general | solution.py:43
  454.4 20.3 %all-to-all-done.2 = bf16[784,2,512]{2,0,1:T(8,128)(2,1)S(1)} async-done(((bf16[784,2,512]{2,0,1:T(8,128)(2,1)}), bf16[784,2,512]{2,0,1:T(8,128)(2,1)S(1)}, u32[]{:S(2)}, u32[]{:S(2)}) %all-to-all-start.2) | async-done | bytes 1605664 | tf_op jit(solution)/shard_map/all_to_all | solution.py:229
  482.8 28.1 %fusion.41 = bf16[1568,1,8,64]{0,3,2,1:T(8,128)(2,1)S(1)} fusion(bf16[1568,8,64]{0,2,1:T(8,128)(2,1)S(1)} %squeeze.39, f32[8,1568,1568]{1,2,0:T(8,128)} %get-tuple-element.96, f32[8,1568]{1,0:T(8,128)S(1)} %log_add_fusion), kind=kOutput, calls=%fused_computation.76 | convolution fusion | flops 2577440768 | bytes 81937408 | tf_op jit(solution)/shard_map/while/body/eval_jaxpr/hqk,qhd->khd/dot_general | solution.py:71
  511.0 56.5 %multiply_reduce_fusion = (f32[8,1568]{1,0:T(8,128)S(1)}, f32[8,1568,1568]{1,2,0:T(8,128)}) fusion(f32[8,1568,1568]{1,2,0:T(8,128)} %get-tuple-element.96, f32[8,1568]{1,0:T(8,128)S(1)} %log_add_fusion, bf16[1568,8,64]{0,2,1:T(8,128)(2,1)S(1)} %squeeze.39, bf16[1568,3,8,64]{0,3,2,1:T(8,128)(2,1)} %squeeze.35), kind=kOutput, calls=%fused_computation.1 | convolution fusion | flops 2596294400 | bytes 165578752 | tf_op jit(solution)/shard_map/while/body/eval_jaxpr/qhd,khd->hqk/dot_general | solution.py:74
  567.5 64.7 %multiply_convert_fusion = bf16[8,1568,1568]{1,2,0:T(8,128)(2,1)} fusion(f32[8,1568,1568]{1,2,0:T(8,128)} %get-tuple-element.101, f32[8,1568,1568]{1,2,0:T(8,128)} %get-tuple-element.96, f32[8,1568]{1,0:T(8,128)S(1)} %get-tuple-element.100, f32[8,1568]{1,0:T(8,128)S(1)} %log_add_fusion), kind=kLoop, calls=%fused_computation | loop fusion | flops 98344960 | bytes 196790272 | tf_op jit(solution)/shard_map/while/body/eval_jaxpr/convert_element_type | solution.py:78
  632.3 19.4 %fusion.40 = bf16[1568,1,8,64]{0,3,2,1:T(8,128)(2,1)S(1)} fusion(bf16[8,1568,1568]{1,2,0:T(8,128)(2,1)} %multiply_convert_fusion, bf16[1568,3,8,64]{0,3,2,1:T(8,128)(2,1)} %squeeze.35), kind=kOutput, calls=%fused_computation.75 | convolution fusion | flops 2519236608 | bytes 45056000 | tf_op jit(solution)/shard_map/while/body/eval_jaxpr/hqk,qhd->khd/dot_general | solution.py:82
  651.7 21.0 %fusion.39 = bf16[1568,1,8,64]{0,3,2,1:T(8,128)(2,1)} fusion(bf16[8,1568,1568]{1,2,0:T(8,128)(2,1)} %multiply_convert_fusion, bf16[1568,3,8,64]{0,3,2,1:T(8,128)(2,1)} %squeeze.35), kind=kOutput, calls=%fused_computation.74 | convolution fusion | flops 2519236608 | bytes 45056000 | tf_op jit(solution)/shard_map/while/body/eval_jaxpr/hqk,khd->qhd/dot_general | solution.py:79
  701.9 48.5 %all-to-all-done.3 = bf16[2,784,3,1,512]{4,1,3,2,0:T(8,128)(2,1)} async-done(((bf16[2,784,3,1,512]{4,1,3,2,0:T(8,128)(2,1)}), bf16[2,784,3,1,512]{4,1,3,2,0:T(8,128)(2,1)}, u32[]{:S(2)}, u32[]{:S(2)}) %all-to-all-start.3) | async-done | bytes 4816928 | tf_op jit(solution)/shard_map/all_to_all | solution.py:239
  784.0 15.1 %convolution_convert_fusion.1 = bf16[1024,4096]{1,0:T(8,128)(2,1)} fusion(bf16[784,4096]{1,0:T(8,128)(2,1)} %get-tuple-element.104, f32[784,1024]{1,0:T(8,128)} %copy-done.5, f32[1024]{0:T(1024)S(1)} %copy-done.32, f32[1024]{0:T(1024)S(1)} %copy-done.23, f32[784]{0:T(1024)S(1)} %copy-done.25, f32[784]{0:T(1024)S(1)} %copy-done.17), kind=kOutput, calls=%fused_computation.38 | convolution fusion | flops 6584877056 | bytes 18036864 | tf_op jit(solution)/shard_map/dot_general | solution.py:37
  799.1 14.7 %convolution_convert_fusion = bf16[4096,1024]{0,1:T(8,128)(2,1)} fusion(bf16[784,4096]{1,0:T(8,128)(2,1)} %get-tuple-element.105, f32[784,1024]{1,0:T(8,128)} %param.29), kind=kOutput, calls=%fused_computation.37 | convolution fusion | flops 6581665792 | bytes 18022400 | tf_op jit(solution)/shard_map/dot_general | solution.py:37
  817.5 47.1 %reduce-scatter.9.cloned.1.call-done = bf16[1024,192]{0,1:T(8,128)(2,1)} async-done(((bf16[1024,3072]{0,1:T(8,128)(2,1)}), bf16[1024,192]{0,1:T(8,128)(2,1)}) %reduce-scatter.9.cloned.1.call-update) | async-done | bytes 393232 | tf_op jit(solution)/shard_map/reduce_scatter | solution.py:274
  880.2 61.5 %all-reduce.34 = (bf16[1024]{0:T(1024)(128)(2,1)S(1)}, bf16[1024]{0:T(1024)(128)(2,1)S(1)}, bf16[1024]{0:T(1024)(128)(2,1)S(1)}, bf16[1024]{0:T(1024)(128)(2,1)S...) all-reduce(bf16[1024]{0:T(1024)(128)(2,1)S(1)} %dynamic-update-slic, ...), channel_id=1, replica_groups=mesh['row'=2,'col'=16] {'col'}, use_global_device_ids=true, to_apply=%add.15 | all-reduce | flops 13312 | bytes 53248
  941.7 30.1 %reduce-scatter.17.cloned.1.call-done = bf16[1024,256]{1,0:T(8,128)(2,1)} async-done(((bf16[1024,4096]{1,0:T(8,128)(2,1)}), bf16[1024,256]{1,0:T(8,128)(2,1)}) %reduce-scatter.17.cloned.1.call-update) | async-done | bytes 524304 | tf_op jit(solution)/shard_map/reduce_scatter | solution.py:280
  994.7 84.3 %reduce-scatter.21.cloned.1.call-done = bf16[4096,64]{0,1:T(8,128)(2,1)} async-done(((bf16[4096,1024]{0,1:T(8,128)(2,1)}), bf16[4096,64]{0,1:T(8,128)(2,1)}) %reduce-scatter.21.cloned.1.call-update) | async-done | bytes 524304 | tf_op jit(solution)/shard_map/reduce_scatter | solution.py:283
  1108.3 15.2 %reduce-scatter.19.cloned.1.call-done = bf16[512,256]{1,0:T(8,128)(2,1)} async-done(((bf16[1024,256]{1,0:T(8,128)(2,1)}), bf16[512,256]{1,0:T(8,128)(2,1)}) %reduce-scatter.19.cloned.1.call-update) | async-done | bytes 262160 | tf_op jit(solution)/shard_map/reduce_scatter | solution.py:335
  1125.3 15.0 %reduce-scatter.23.cloned.1.call-done = bf16[2048,64]{0,1:T(8,128)(2,1)} async-done(((bf16[4096,64]{0,1:T(8,128)(2,1)}), bf16[2048,64]{0,1:T(8,128)(2,1)}) %reduce-scatter.23.cloned.1.call-update) | async-done | bytes 262160 | tf_op jit(solution)/shard_map/reduce_scatter | solution.py:338
  (238 shorter events, 287.9 us)
Async XLA Ops:
  7.2 102.9 %copy-start = (bf16[784,1024]{1,0:T(8,128)(2,1)S(1)}, bf16[784,1024]{1,0:T(8,128)(2,1)}, u32[]{:S(2)}) copy-start(bf16[784,1024]{1,0:T(8,128)(2,1)} %param.15) | copy-start | bytes 4816900
  7.2 103.6 %all-gather.7.cloned.1.call-start = ((), (), s32[]{:S(2)}) async-start(), calls=%async_computation.12 | async-start | bytes 6684672 | tf_op jit(solution)/shard_map/all_gather | solution.py:149
  17.9 354.0 %all-gather.9.cloned.1.call-start = ((), (), s32[]{:S(2)}) async-start(), calls=%async_computation.13 | async-start | bytes 2228224 | tf_op jit(solution)/shard_map/all_gather | solution.py:150
  23.2 355.0 %all-gather.11.cloned.1.call-start = ((), (), s32[]{:S(2)}) async-start(), calls=%async_computation.14 | async-start | bytes 8912896 | tf_op jit(solution)/shard_map/all_gather | solution.py:151
  138.3 61.4 %all-to-all-start = ((bf16[784,3,2,512]{3,0,1,2:T(8,128)(2,1)}), bf16[784,3,2,512]{3,0,1,2:T(8,128)(2,1)}, u32[]{:S(2)}, u32[]{:S(2)}) async-start(bf16[784,3,2,512]{3,0,1,2:T(8,128)(2,1)} %copy.59), calls=%async_computation | async-start | bytes 9633792 | tf_op jit(solution)/shard_map/all_to_all | solution.py:178
  144.3 273.0 %all-gather.13.cloned.1.call-start = ((), (), s32[]{:S(2)}) async-start(), calls=%async_computation.15 | async-start | bytes 8912896 | tf_op jit(solution)/shard_map/all_gather | solution.py:152
  258.0 26.7 %copy-start.9 = (f32[8,1568]{1,0:T(8,128)}, f32[8,1568]{1,0:T(8,128)S(1)}, u32[]{:S(2)}) copy-start(f32[8,1568]{1,0:T(8,128)S(1)} %get-tuple-element.95) | copy-start | bytes 150532
  284.8 30.6 %copy-start.12 = (f32[8,1568]{1,0:T(8,128)}, f32[8,1568]{1,0:T(8,128)S(1)}, u32[]{:S(2)}) copy-start(f32[8,1568]{1,0:T(8,128)S(1)} %fusion) | copy-start | bytes 150532
  321.4 43.3 %all-to-all-start.1 = ((bf16[2,2,200704]{2,1,0:T(2,128)(2,1)}), bf16[2,2,200704]{2,1,0:T(2,128)(2,1)S(1)}, u32[]{:S(2)}, u32[]{:S(2)}) async-start(bf16[2,2,200704]{2,1,0:T(2,128)(2,1)} %reshape.232), calls=%async_computation.1 | async-start | bytes 3211264 | tf_op jit(solution)/shard_map/all_to_all | solution.py:183
  325.1 120.4 %copy-start.22 = (f32[1024]{0:T(1024)}, f32[1024]{0:T(1024)S(1)}, u32[]{:S(2)}) copy-start(f32[1024]{0:T(1024)S(1)} %convert_element_type.193) | copy-start | bytes 12292
  325.1 53.1 %copy-start.31 = (f32[1024]{0:T(1024)}, f32[1024]{0:T(1024)S(1)}, u32[]{:S(2)}) copy-start(f32[1024]{0:T(1024)S(1)} %convert_element_type.194) | copy-start | bytes 12292
  376.0 69.5 %copy-start.16 = (f32[784]{0:T(1024)}, f32[784]{0:T(1024)S(1)}, u32[]{:S(2)}) copy-start(f32[784]{0:T(1024)S(1)} %broadcast_multiply_fusion.4) | copy-start | bytes 9412
  378.2 67.3 %copy-start.24 = (f32[784]{0:T(1024)}, f32[784]{0:T(1024)S(1)}, u32[]{:S(2)}) copy-start(f32[784]{0:T(1024)S(1)} %add_rsqrt_fusion) | copy-start | bytes 9412
  378.2 39.0 %copy-start.7 = (f32[784,1024]{1,0:T(8,128)S(1)}, f32[784,1024]{1,0:T(8,128)}, u32[]{:S(2)}) copy-start(f32[784,1024]{1,0:T(8,128)} %param.29) | copy-start | bytes 9633796
  450.7 24.0 %all-to-all-start.2 = ((bf16[784,2,512]{2,0,1:T(8,128)(2,1)}), bf16[784,2,512]{2,0,1:T(8,128)(2,1)S(1)}, u32[]{:S(2)}, u32[]{:S(2)}) async-start(bf16[784,2,512]{2,0,1:T(8,128)(2,1)} %bitcast.88), calls=%async_computation.2 | async-start | bytes 3211264 | tf_op jit(solution)/shard_map/all_to_all | solution.py:229
  690.3 60.1 %all-to-all-start.3 = ((bf16[2,784,3,1,512]{4,1,3,2,0:T(8,128)(2,1)}), bf16[2,784,3,1,512]{4,1,3,2,0:T(8,128)(2,1)}, u32[]{:S(2)}, u32[]{:S(2)}) async-start(bf16[2,784,3,1,512]{4,1,3,2,0:T(8,128)(2,1)} %pad_maximum_fusion.1), calls=%async_computation.3 | async-start | bytes 9633792 | tf_op jit(solution)/shard_map/all_to_all | solution.py:239
  696.4 117.5 %reduce-scatter.13.cloned.1.call-start = ((), (), s32[]{:S(2)}) async-start(), calls=%async_computation.18 | async-start | bytes 2228224 | tf_op jit(solution)/shard_map/reduce_scatter | solution.py:277
  701.6 163.0 %reduce-scatter.9.cloned.1.call-start = ((), (), s32[]{:S(2)}) async-start(), calls=%async_computation.16 | async-start | bytes 6684672 | tf_op jit(solution)/shard_map/reduce_scatter | solution.py:274
  783.3 188.5 %reduce-scatter.17.cloned.1.call-start = ((), (), s32[]{:S(2)}) async-start(), calls=%async_computation.20 | async-start | bytes 8912896 | tf_op jit(solution)/shard_map/reduce_scatter | solution.py:280
  799.1 279.9 %reduce-scatter.21.cloned.1.call-start = ((), (), s32[]{:S(2)}) async-start(), calls=%async_computation.22 | async-start | bytes 8912896 | tf_op jit(solution)/shard_map/reduce_scatter | solution.py:283
  813.9 277.4 %reduce-scatter.15.cloned.1.call-start = ((), (), s32[]{:S(2)}) async-start(), calls=%async_computation.19 | async-start | bytes 196608 | tf_op jit(solution)/shard_map/reduce_scatter | solution.py:332
  814.6 292.0 %reduce-scatter.11.cloned.1.call-start = ((), (), s32[]{:S(2)}) async-start(), calls=%async_computation.17 | async-start | bytes 589824 | tf_op jit(solution)/shard_map/reduce_scatter | solution.py:329
  864.6 258.9 %reduce-scatter.19.cloned.1.call-start = ((), (), s32[]{:S(2)}) async-start(), calls=%async_computation.21 | async-start | bytes 786432 | tf_op jit(solution)/shard_map/reduce_scatter | solution.py:335
  971.9 168.4 %reduce-scatter.23.cloned.1.call-start = ((), (), s32[]{:S(2)}) async-start(), calls=%async_computation.23 | async-start | bytes 786432 | tf_op jit(solution)/shard_map/reduce_scatter | solution.py:338
  (34 other events, 215.4 us)
Sparse Core Ops, SparseCore 0:
  18.0 62.1 all-gather.6
  82.3 40.4 all-gather.8
  125.0 76.9 all-gather.10
  204.0 72.4 all-gather.12
  701.7 59.4 reduce-scatter.12
  783.4 81.1 reduce-scatter.8
  868.7 103.1 reduce-scatter.16
  975.9 103.0 reduce-scatter.20
  1081.2 9.9 reduce-scatter.14
  1093.3 13.1 reduce-scatter.10
  1108.8 14.6 reduce-scatter.18
  1125.6 14.6 reduce-scatter.22
